TPU v7x, 128 devices: a whole 4x4x4 slice. The times are simulated.
128 devices in a mesh: blk: 8 (over z_lo, y), tile: 16 (over x, z_hi, core).
Axes of the slice: x: 4, y: 4, z: 4 (z_hi: 2, z_lo: 2; z = z_hi * 2 + z_lo), core: 2. Of those that a mesh axis runs over, the one named last changes fastest.
Arguments:
- left_rows: bfloat16 [2048, 49152], P('blk', 'tile'), may hold values from -0.125 to 0.125
- right_rows: bfloat16 [2048, 4096], P('blk', 'tile'), may hold values from -6 to 6
- row_weight: float32 [2048], P('blk'), may hold values from 0.25 to 4
- coupling: float32 [2048], P('blk'), may hold values from -6 to 6
- assign: int32 [16], replicated, may hold values from 0 to 7, as said below
- orders: int32 [16], replicated, may hold values from 42 to 214, as said below
- offsets: int32 [16], replicated, may hold values from 0 to 214, as said below
Outputs:
- schur_band: bfloat16 [4096, 49152], P('blk', 'tile')
Inputs may be any that keep to these rules, and one draw needn't show every extreme that they name: `assign`: each blk index names exactly 2 blocks. The orders of the blocks that one blk index names sum to at most 256, and to exactly 256 for some index in every draw. offsets[b] is the sum of the orders of the blocks before b in the list that name the same blk index.
All inputs are finite; a program needn't handle non-finite values.
Results may differ from a plain program's by a relative error of at most 0.013.
Values may be sent and summed in bfloat16 or wider, within the bound.
A program may use at most 128 MiB of HBM per device.

v0:
```python
import jax
import jax.numpy as jnp
from jax import lax
from jax.sharding import PartitionSpec as P

BAND = 4096


def weigh_rows(right_rows, row_weight, coupling, member, orders):
    right_wide = right_rows.astype(jnp.float32)
    block_sums = jnp.dot(member.T, coupling[:, None] * right_wide, precision=lax.Precision.HIGHEST)
    block_terms = block_sums / jnp.sqrt(orders.astype(jnp.float32))[:, None]
    spread_back = jnp.dot(member, block_terms, precision=lax.Precision.HIGHEST)
    is_live = jnp.sum(member, axis=1, keepdims=True)
    return (is_live * row_weight[:, None] * right_wide + coupling[:, None] * spread_back).astype(
        jnp.bfloat16
    )


def contract(cols_piece, slab_left):
    return lax.dot_general(
        cols_piece, slab_left, (((0,), (0,)), ((), ())), preferred_element_type=jnp.float32
    )


def shards(left_rows, right_rows, row_weight, coupling, assign, orders, offsets):
    height = left_rows.shape[0]
    my_index = lax.axis_index("blk")
    row_ids = lax.broadcasted_iota(jnp.int32, (height, assign.shape[0]), 0)
    member = (
        (assign[None, :] == my_index)
        & (row_ids >= offsets[None, :])
        & (row_ids < offsets[None, :] + orders[None, :])
    ).astype(jnp.float32)
    weighted = weigh_rows(right_rows, row_weight, coupling, member, orders)
    weighted_all = lax.all_gather(weighted, "tile", axis=1, tiled=True)
    block_width = min(512, BAND)

    def one_block(first_col):
        cols_piece = lax.dynamic_slice_in_dim(weighted_all, first_col, block_width, 1)
        return contract(cols_piece, left_rows).astype(jnp.bfloat16)

    starts = jnp.arange(BAND // block_width, dtype=jnp.int32) * block_width
    partials = lax.map(one_block, starts).reshape(BAND, left_rows.shape[1])
    result = lax.psum_scatter(partials, "blk", scatter_dimension=0, tiled=True).astype(jnp.float32)
    return result.astype(jnp.bfloat16)


def solution(mesh):
    return jax.shard_map(
        shards,
        mesh=mesh,
        in_specs=(P("blk", "tile"), P("blk", "tile"), P("blk"), P("blk"), P(), P(), P()),
        out_specs=P("blk", "tile"),
        check_vma=False,
    )
```

profile of v0, /device:TPU:0, one launch (start us, length us, event | category | flops | bytes accessed | tf_op | source)
XLA Modules:
  0.0 376.2 jit_solution(2312812126691076642)
XLA Ops:
  6.5 0.7 convert_sqrt_fusion
  7.2 0.7 add.15
  7.9 0.7 broadcast_compare_fusion
  8.5 0.7 convert_reduce_fusion
  9.3 0.7 mul.30
  10.0 1.2 convolution_divide_fusion
  11.1 2.0 fusion.5
  13.2 52.1 %all-gather.2.cloned.1.call-done = bf16[256,4096]{1,0:T(8,128)(2,1)} async-done(((bf16[256,256]{1,0:T(8,128)(2,1)}), bf16[256,4096]{1,0:T(8,128)(2,1)}) %all-gather.2.cloned.1.call-update) | async-done | bytes 2097168 | tf_op jit(solution)/shard_map/all_gather | solution.py:36
  65.3 54.9 %while.10 = (s32[]{:T(128)}, bf16[8,512,3072]{2,1,0:T(8,128)(2,1)}, s32[8]{0:T(128)S(1)}, bf16[256,4096]{1,0:T(8,128)(2,1)}, bf16[256,3072]{1,0:T(8,128)(2,1)}, /*index=5*/s32[]{:T(128)}, s32[]{:T(128)}, s32[]{:T(128)}) while((s32[]{:T(128)}, bf16[8,512,3072]{2,1,0:T(8,128)(2,1)}, s32[8]{0:T(128)S(1)}, bf16[256,4096]{1,0:T(8,128)(2,1)}, ...), condition=%wide.region_2.3_spmd, body=%wide.region_1.2_spmd.sunk | while | flops 806879232 | bytes 4980883 | solution.py:44
  65.3 0.6 dynamic_slice.12
  67.8 4.3 %fusion.18 = bf16[8,512,3072]{2,1,0:T(8,128)(2,1)} fusion(bf16[8,512,3072]{2,1,0:T(8,128)(2,1)} %get-tuple-element.83, s32[]{:T(128)S(6)} %copy.11, bf16[256,3072]{1,0:T(8,128)(2,1)} %get-tuple-element.94, bf16[256,4096]{1,0:T(8,128)(2,1)} %get-tuple-element.93, s32[]{:T(128)S(6)} %select_n.4), kind=kOutput, calls=%fused_computation.2.clone.1 | convolution fusion | flops 806879232 | bytes 4980744 | tf_op jit(solution)/shard_map/while/body/eval_jaxpr/dot_general | solution.py:21
  72.2 0.6 dynamic_slice.12
  74.7 4.4 %fusion.18 = bf16[8,512,3072]{2,1,0:T(8,128)(2,1)} fusion(bf16[8,512,3072]{2,1,0:T(8,128)(2,1)} %get-tuple-element.83, s32[]{:T(128)S(6)} %copy.11, bf16[256,3072]{1,0:T(8,128)(2,1)} %get-tuple-element.94, bf16[256,4096]{1,0:T(8,128)(2,1)} %get-tuple-element.93, s32[]{:T(128)S(6)} %select_n.4), kind=kOutput, calls=%fused_computation.2.clone.1 | convolution fusion | flops 806879232 | bytes 4980744 | tf_op jit(solution)/shard_map/while/body/eval_jaxpr/dot_general | solution.py:21
  79.1 0.6 dynamic_slice.12
  81.6 4.4 %fusion.18 = bf16[8,512,3072]{2,1,0:T(8,128)(2,1)} fusion(bf16[8,512,3072]{2,1,0:T(8,128)(2,1)} %get-tuple-element.83, s32[]{:T(128)S(6)} %copy.11, bf16[256,3072]{1,0:T(8,128)(2,1)} %get-tuple-element.94, bf16[256,4096]{1,0:T(8,128)(2,1)} %get-tuple-element.93, s32[]{:T(128)S(6)} %select_n.4), kind=kOutput, calls=%fused_computation.2.clone.1 | convolution fusion | flops 806879232 | bytes 4980744 | tf_op jit(solution)/shard_map/while/body/eval_jaxpr/dot_general | solution.py:21
  86.0 0.6 dynamic_slice.12
  88.5 4.3 %fusion.18 = bf16[8,512,3072]{2,1,0:T(8,128)(2,1)} fusion(bf16[8,512,3072]{2,1,0:T(8,128)(2,1)} %get-tuple-element.83, s32[]{:T(128)S(6)} %copy.11, bf16[256,3072]{1,0:T(8,128)(2,1)} %get-tuple-element.94, bf16[256,4096]{1,0:T(8,128)(2,1)} %get-tuple-element.93, s32[]{:T(128)S(6)} %select_n.4), kind=kOutput, calls=%fused_computation.2.clone.1 | convolution fusion | flops 806879232 | bytes 4980744 | tf_op jit(solution)/shard_map/while/body/eval_jaxpr/dot_general | solution.py:21
  92.8 0.6 dynamic_slice.12
  95.3 4.3 %fusion.18 = bf16[8,512,3072]{2,1,0:T(8,128)(2,1)} fusion(bf16[8,512,3072]{2,1,0:T(8,128)(2,1)} %get-tuple-element.83, s32[]{:T(128)S(6)} %copy.11, bf16[256,3072]{1,0:T(8,128)(2,1)} %get-tuple-element.94, bf16[256,4096]{1,0:T(8,128)(2,1)} %get-tuple-element.93, s32[]{:T(128)S(6)} %select_n.4), kind=kOutput, calls=%fused_computation.2.clone.1 | convolution fusion | flops 806879232 | bytes 4980744 | tf_op jit(solution)/shard_map/while/body/eval_jaxpr/dot_general | solution.py:21
  99.7 0.6 dynamic_slice.12
  102.2 4.3 %fusion.18 = bf16[8,512,3072]{2,1,0:T(8,128)(2,1)} fusion(bf16[8,512,3072]{2,1,0:T(8,128)(2,1)} %get-tuple-element.83, s32[]{:T(128)S(6)} %copy.11, bf16[256,3072]{1,0:T(8,128)(2,1)} %get-tuple-element.94, bf16[256,4096]{1,0:T(8,128)(2,1)} %get-tuple-element.93, s32[]{:T(128)S(6)} %select_n.4), kind=kOutput, calls=%fused_computation.2.clone.1 | convolution fusion | flops 806879232 | bytes 4980744 | tf_op jit(solution)/shard_map/while/body/eval_jaxpr/dot_general | solution.py:21
  109.1 4.4 %fusion.18 = bf16[8,512,3072]{2,1,0:T(8,128)(2,1)} fusion(bf16[8,512,3072]{2,1,0:T(8,128)(2,1)} %get-tuple-element.83, s32[]{:T(128)S(6)} %copy.11, bf16[256,3072]{1,0:T(8,128)(2,1)} %get-tuple-element.94, bf16[256,4096]{1,0:T(8,128)(2,1)} %get-tuple-element.93, s32[]{:T(128)S(6)} %select_n.4), kind=kOutput, calls=%fused_computation.2.clone.1 | convolution fusion | flops 806879232 | bytes 4980744 | tf_op jit(solution)/shard_map/while/body/eval_jaxpr/dot_general | solution.py:21
  116.0 4.3 %fusion.18 = bf16[8,512,3072]{2,1,0:T(8,128)(2,1)} fusion(bf16[8,512,3072]{2,1,0:T(8,128)(2,1)} %get-tuple-element.83, s32[]{:T(128)S(6)} %copy.11, bf16[256,3072]{1,0:T(8,128)(2,1)} %get-tuple-element.94, bf16[256,4096]{1,0:T(8,128)(2,1)} %get-tuple-element.93, s32[]{:T(128)S(6)} %select_n.4), kind=kOutput, calls=%fused_computation.2.clone.1 | convolution fusion | flops 806879232 | bytes 4980744 | tf_op jit(solution)/shard_map/while/body/eval_jaxpr/dot_general | solution.py:21
  120.3 249.0 %reduce-scatter.2.cloned.1.call-done = bf16[512,3072]{1,0:T(8,128)(2,1)} async-done(((bf16[4096,3072]{1,0:T(8,128)(2,1)}), bf16[512,3072]{1,0:T(8,128)(2,1)}) %reduce-scatter.2.cloned.1.call-update) | async-done | bytes 3145744 | tf_op jit(solution)/shard_map/reduce_scatter | solution.py:45
  (8 shorter events, 1.2 us)
Async XLA Ops:
  6.5 58.8 %all-gather.2.cloned.1.call-start = ((), (), s32[]{:S(2)}) async-start(), calls=%async_computation.1 | async-start | bytes 2228224 | tf_op jit(solution)/shard_map/all_gather | solution.py:36
  13.2 356.2 %reduce-scatter.2.cloned.1.call-start = ((), (), s32[]{:S(2)}) async-start(), calls=%async_computation.2 | async-start | bytes 28311552 | tf_op jit(solution)/shard_map/reduce_scatter | solution.py:45
Sparse Core Ops, SparseCore 0:
  13.3 51.9 all-gather.1
  120.4 248.8 reduce-scatter.1
where the time goes:
time: 377 us; the launch traced here: 376 us
  waiting for transfers between devices  301 us (80%)
  matrix products  37.9 us (10%)
  loops' own time  15.6 us (4%)
  between operations  13.4 us (4%)
  local copies, waits for them, and re-layouts  4.66 us (1%)
    reduce_scatter x1, waiting for transfers between devices, shards(): lax.psum_scatter(partials, 'blk', scatter_dimension=0, tiled=True)  249 us
    all_gather x1, waiting for transfers between devices, shards(): weighted_all = lax.all_gather(weighted, 'tile', axis=1, tiled=True)  52.1 us
    dot_general x8, matrix products, contract(): lax.dot_general(cols_piece, slab_left, (((0,), (0,)), ((), ())), preferre...  34.7 us
    another operation x1, loops' own time, shards(): partials = lax.map(one_block, starts).reshape(BAND, left_rows.shape[1])  15.6 us
  transfers between devices with their start and end apart: 2, of which 2 were waited for; matrix products, arithmetic and copies ran while one was open for 0% of the time, Pallas kernels for 0%

commit v1 on v0

v1 whole, which is shorter than its diff:
```python
import functools

import jax
import jax.numpy as jnp
from jax import lax
from jax.experimental import pallas as pl
from jax.experimental.pallas import tpu as pltpu
from jax.sharding import PartitionSpec as P

MESH = pl.DeviceIdType.MESH
F32 = jnp.float32
BF16 = jnp.bfloat16
HIGH = lax.Precision.HIGHEST
PLANS = 3
STEPS = 4


def flip(bit):
    return 1 - bit


def differ(one, other):
    return (one + other) % 2


def ring_bits(place):
    high = place // 2
    return (place + high) % 2, high


def ring_place(low, high):
    return 2 * high + (low + high) % 2


def blk_bits(index):
    low, high = ring_bits(index % 4)
    return low, high, index // 4


def blk_index(bits):
    return bits[2] * 4 + ring_place(bits[0], bits[1])


def weigh(mine, assign, orders, offsets, row_weight, coupling, right):
    n_rows = right.shape[0]
    n_blocks = assign.shape[0]
    slots = lax.broadcasted_iota(jnp.int32, (1, n_rows), 1)
    members, scaled = [], []
    for block in range(n_blocks):
        start = offsets[block]
        inside = (
            (jnp.full((1, n_rows), assign[block], jnp.int32) == mine)
            & (slots >= start)
            & (slots < start + orders[block])
        ).astype(F32)
        members.append(inside)
        scaled.append(inside / jnp.sqrt(jnp.full((1, n_rows), orders[block], jnp.int32).astype(F32)))
    member = jnp.concatenate(members, axis=0)
    shares = jnp.concatenate(scaled, axis=0)
    right_t = right[...].astype(F32).T
    sums = lax.dot_general(
        right_t * coupling[...], member, (((1,), (1,)), ((), ())), precision=HIGH, preferred_element_type=F32
    )
    spread = lax.dot_general(
        sums, shares, (((1,), (0,)), ((), ())), precision=HIGH, preferred_element_type=F32
    )
    live = jnp.sum(member, axis=0, keepdims=True)
    return (live * row_weight[...] * right_t + coupling[...] * spread).astype(BF16)


def kernel(
    assign, orders, offsets, row_weight, coupling, right, left, out,
    slabs, weights, piece, partial, arrived, total, final,
    own_send, own_recv, fwd_send, fwd_recv, sum_send, sum_recv,
    local_sem, put_send, put_recv, x_send, x_recv, xf_send, xf_recv, core_send, core_recv, out_sem,
):
    height, width = left.shape
    plan_width = width // PLANS
    step_width = plan_width // STEPS
    half = height // 2
    block = weights.shape[2]
    core_rows = block // 2
    x_rows = core_rows // 4
    blk = lax.axis_index("blk")
    tile = lax.axis_index("tile")
    x, z_hi, core = tile // 4, (tile // 2) % 2, tile % 2
    bits = blk_bits(blk)
    x_bits = ring_bits(x)

    def across(dim):
        return blk_index([flip(bit) if at == dim else bit for at, bit in enumerate(bits)])

    def beside(dim):
        place = ring_place(*[flip(bit) if at == dim else bit for at, bit in enumerate(x_bits)])
        return place * 4 + z_hi * 2 + core

    def remote(src, dst, send, recv, blk_to, tile_to):
        return pltpu.make_async_remote_copy(
            src_ref=src, dst_ref=dst, send_sem=send, recv_sem=recv,
            device_id=(blk_to, tile_to), device_id_type=MESH,
        )

    def columns(plan, step):
        return pl.ds(pl.multiple_of(plan * plan_width + step * step_width, step_width), step_width)

    def own_copy(plan, step, side):
        cols = columns(plan, step)
        return remote(
            left.at[:, cols], slabs.at[1 + side, :, cols],
            own_send.at[plan, step, side], own_recv.at[plan, step, side],
            across((plan + 1 + side) % 3), tile,
        )

    def fwd_copy(plan, step, side):
        cols = columns(plan, step)
        rows = pl.ds(side * half, half)
        return remote(
            slabs.at[2 - side, rows, cols], slabs.at[3, rows, cols],
            fwd_send.at[plan, step, side], fwd_recv.at[plan, step, side],
            across((plan + 1 + side) % 3), tile,
        )

    def sum_copy(plan, step):
        cols = columns(plan, step)
        return remote(
            partial.at[:, cols], arrived.at[:, cols],
            sum_send.at[plan, step], sum_recv.at[plan, step], across(plan), tile,
        )

    local = pltpu.make_async_copy(left, slabs.at[0], local_sem)
    local.start()

    def send_own(step):
        for plan in range(PLANS):
            for side in range(2):
                own_copy(plan, step, side).start()

    send_own(0)

    piece[...] = weigh(blk, assign, orders, offsets, row_weight, coupling, right)
    band_bits = blk_bits(2 * x + z_hi)

    def put(plan):
        q, r = (plan + 1) % 3, (plan + 2) % 3
        goal = blk_index([bits[at] if at == plan else band_bits[at] for at in range(3)])
        kind = differ(band_bits[plan], bits[plan])
        slot = differ(band_bits[q], bits[q]) + 2 * differ(band_bits[r], bits[r])
        lanes = pl.ds(pl.multiple_of(slot * height, height), height)
        for x_to in range(4):
            for z_to in range(2):
                goal_tile = x_to * 4 + z_to * 2 + core
                rows = pl.ds(pl.multiple_of(core * core_rows + x_to * x_rows, x_rows), x_rows)
                src = piece.at[pl.ds(x_to * x_rows, x_rows), :]
                dst = weights.at[plan, kind, rows, lanes]
                stays = (goal == blk) & (goal_tile == tile)
                yield stays, src, dst, goal, goal_tile, put_send.at[plan, x_to, z_to], put_recv.at[plan]

    for plan in range(PLANS):
        for stays, src, dst, goal, goal_tile, send, recv in put(plan):
            @pl.when(stays)
            def _():
                pltpu.make_async_copy(src, dst, recv).start()

            @pl.when(jnp.logical_not(stays))
            def _():
                remote(src, dst, send, recv, goal, goal_tile).start()

    for step in range(1, STEPS):
        send_own(step)

    def x_region(plan, x_from, first, count):
        start = pl.multiple_of(core * core_rows + x_from * x_rows + first, count)
        return weights.at[plan, :, pl.ds(start, count), :]

    x_near = [ring_place(flip(x_bits[0]), x_bits[1]), ring_place(x_bits[0], flip(x_bits[1]))]
    x_far = ring_place(flip(x_bits[0]), flip(x_bits[1]))

    def x_copy(plan, side):
        region = x_region(plan, x, 0, x_rows)
        return remote(region, region, x_send.at[plan, side], x_recv.at[plan, side], blk, beside(side))

    def xf_copy(plan, side):
        region = x_region(plan, x_near[1 - side], side * (x_rows // 2), x_rows // 2)
        return remote(region, region, xf_send.at[plan, side], xf_recv.at[plan, side], blk, beside(side))

    def core_copy(plan, index, x_from):
        region = x_region(plan, x_from, 0, x_rows)
        return remote(
            region, region, core_send.at[plan, index], core_recv.at[plan, index], blk, tile + 1 - 2 * core
        )

    order = [x, x_near[0], x_near[1], x_far]
    for plan in range(PLANS):
        region = x_region(plan, x, 0, x_rows)
        pltpu.make_async_copy(region, region, put_recv.at[plan]).wait()
        for side in range(2):
            x_copy(plan, side).start()
        core_copy(plan, 0, order[0]).start()

    def forward(step):
        for plan in range(PLANS):
            for side in range(2):
                own_copy(plan, step, side).wait_recv()
            for side in range(2):
                fwd_copy(plan, step, side).start()

    forward(0)
    for plan in range(PLANS):
        for side in range(2):
            x_copy(plan, side).wait_recv()
        for side in range(2):
            xf_copy(plan, side).start()
        for side in range(2):
            core_copy(plan, 1 + side, order[1 + side]).start()
    for step in range(1, STEPS):
        forward(step)
    for plan in range(PLANS):
        for side in range(2):
            xf_copy(plan, side).wait_recv()
        core_copy(plan, 3, order[3]).start()
    for plan in range(PLANS):
        for index in range(4):
            core_copy(plan, index, order[index]).wait_recv()
    local.wait()

    def product(plan, kind, cols):
        rows = slabs[:, :, cols].reshape(4 * height, step_width)
        return jnp.dot(weights[plan, kind], rows, preferred_element_type=F32)

    @pl.loop(0, STEPS)
    def _(step):
        for plan in range(PLANS):
            cols = columns(plan, step)
            for side in range(2):
                fwd_copy(plan, step, side).wait_recv()
            partial[:, cols] = product(plan, 1, cols).astype(BF16)
            sum_copy(plan, step).start()
        for plan in range(PLANS):
            cols = columns(plan, step)
            total[:, cols] = product(plan, 0, cols)

    def out_copy(plan, step):
        cols = columns(plan, step)
        return pltpu.make_async_copy(final.at[:, cols], out.at[:, cols], out_sem.at[plan, step])

    @pl.loop(0, STEPS)
    def _(step):
        for plan in range(PLANS):
            cols = columns(plan, step)
            sum_copy(plan, step).wait_recv()
            final[:, cols] = (total[:, cols] + arrived[:, cols].astype(F32)).astype(BF16)
            out_copy(plan, step).start()

    for plan in range(PLANS):
        for stays, src, dst, goal, goal_tile, send, recv in put(plan):
            @pl.when(jnp.logical_not(stays))
            def _():
                remote(src, dst, send, recv, goal, goal_tile).wait_send()
        for side in range(2):
            x_copy(plan, side).wait_send()
            xf_copy(plan, side).wait_send()
        for index in range(4):
            core_copy(plan, index, order[index]).wait_send()

    @pl.loop(0, STEPS)
    def _(step):
        for plan in range(PLANS):
            for side in range(2):
                own_copy(plan, step, side).wait_send()
                fwd_copy(plan, step, side).wait_send()
            sum_copy(plan, step).wait_send()
            out_copy(plan, step).wait()


def shards(left_rows, right_rows, row_weight, coupling, assign, orders, offsets):
    height, width = left_rows.shape
    band = right_rows.shape[1] * lax.axis_size("tile")
    block = band // lax.axis_size("blk")
    dma = pltpu.SemaphoreType.DMA
    smem = pl.BlockSpec(memory_space=pltpu.SMEM)
    vmem = pl.BlockSpec(memory_space=pltpu.VMEM)
    hbm = pl.BlockSpec(memory_space=pl.ANY)
    return pl.pallas_call(
        kernel,
        out_shape=jax.ShapeDtypeStruct((block, width), BF16),
        in_specs=[smem, smem, smem, vmem, vmem, vmem, hbm],
        out_specs=hbm,
        scratch_shapes=[
            pltpu.VMEM((4, height, width), BF16),
            pltpu.VMEM((PLANS, 2, block, 4 * height), BF16),
            pltpu.VMEM((right_rows.shape[1], height), BF16),
            pltpu.VMEM((block, width), BF16),
            pltpu.VMEM((block, width), BF16),
            pltpu.VMEM((block, width), F32),
            pltpu.VMEM((block, width), BF16),
            dma((PLANS, STEPS, 2)), dma((PLANS, STEPS, 2)),
            dma((PLANS, STEPS, 2)), dma((PLANS, STEPS, 2)),
            dma((PLANS, STEPS)), dma((PLANS, STEPS)),
            dma, dma((PLANS, 4, 2)), dma((PLANS,)),
            dma((PLANS, 2)), dma((PLANS, 2)),
            dma((PLANS, 2)), dma((PLANS, 2)),
            dma((PLANS, 4)), dma((PLANS, 4)),
            dma((PLANS, STEPS)),
        ],
        compiler_params=pltpu.CompilerParams(has_side_effects=True, vmem_limit_bytes=60 * 2**20),
    )(
        assign, orders, offsets, row_weight.reshape(1, height), coupling.reshape(1, height), right_rows, left_rows
    )


def solution(mesh):
    return jax.shard_map(
        shards,
        mesh=mesh,
        in_specs=(P("blk", "tile"), P("blk", "tile"), P("blk"), P("blk"), P(), P(), P()),
        out_specs=P("blk", "tile"),
        check_vma=False,
    )
```

time: 377 us -> 93.4 us (0.25)
  waiting for transfers between devices: 301 us -> 0 us
  Pallas kernels: 0 us -> 88 us
  matrix products: 37.9 us -> 0 us
  loops' own time: 15.6 us -> 0 us
  between operations: 13.4 us -> 0.01 us
    reduce_scatter x1 -> x0, waiting for transfers between devices: 249 us -> none  [shards(): lax.psum_scatter(partials, 'blk', scatter_dimension=0, tiled=True)]
    pallas_call x0 -> x1, Pallas kernels: none -> 88 us  [shards(): pl.pallas_call(kernel, out_shape=jax.ShapeDtypeStruct((block, width), BF1...]
    all_gather x1 -> x0, waiting for transfers between devices: 52.1 us -> none  [shards(): weighted_all = lax.all_gather(weighted, 'tile', axis=1, tiled=True)]
    dot_general x10 -> x0, matrix products: 37.9 us -> none  [the longest x8 34.7 us: contract(): lax.dot_general(cols_piece, slab_left, (((0,), (0,)), ((), ())), preferre...]
    another operation x1 -> x0, loops' own time: 15.6 us -> none  [shards(): partials = lax.map(one_block, starts).reshape(BAND, left_rows.shape[1])]
    dynamic_slice x8 -> x0, local copies, waits for them, and re-layouts: 4.66 us -> none  [shards(): partials = lax.map(one_block, starts).reshape(BAND, left_rows.shape[1])]
  transfers between devices with their start and end apart: 2 -> 0, of which waited for: 2 -> 0; matrix products, arithmetic and copies ran while one was open for 0% -> 0% of each run, Pallas kernels for 0% -> 0%
where the time goes in v1:
time: 93.4 us; the launch traced here: 91.8 us
  Pallas kernels  88 us (94%)
  local copies, waits for them, and re-layouts  3.76 us (4%)
    pallas_call x1, Pallas kernels, shards(): pl.pallas_call(kernel, out_shape=jax.ShapeDtypeStruct((block, width), BF1...  88 us
    unnamed x1, local copies, waits for them, and re-layouts  3.76 us

profile of v1, /device:TPU:0, one launch (start us, length us, event | category | flops | bytes accessed | tf_op | source)
XLA Modules:
  0.0 91.8 jit_solution(11967183088890778896)
XLA Ops:
  0.0 88.0 %shard_map.73 = bf16[512,3072]{1,0:T(8,128)(2,1)} custom-call(s32[16]{0:T(128)} %assign.1, s32[16]{0:T(128)} %orders.1, s32[16]{0:T(128)} %offsets.1, f32[1,256]{1,0:T(1,128)} %bitcast.2, f32[1,256]{1,0:T(1,128)} %bitcast.3, bf16[256,256]{1,0:T(8,128)(2,1)} %right.1, bf16[256,3072]{1,0:T(8,128)(2,1)} %left.1), custom_call_target="tpu_custom_call" | custom-call | tf_op jit(solution)/shard_map/pallas_call | solution.py:283
  88.0 3.8 %copy.9 = bf16[512,3072]{1,0:T(8,128)(2,1)} copy(bf16[512,3072]{1,0:T(8,128)(2,1)} %shard_map.73) | data formatting | bytes 6291456

commit v2 on v1

v2 whole, which is shorter than its diff:
```python
import functools

import jax
import jax.numpy as jnp
from jax import lax
from jax.experimental import pallas as pl
from jax.experimental.pallas import tpu as pltpu
from jax.sharding import PartitionSpec as P

MESH = pl.DeviceIdType.MESH
F32 = jnp.float32
BF16 = jnp.bfloat16
HIGH = lax.Precision.HIGHEST
PLANS = 3
STEPS = 4


def flip(bit):
    return 1 - bit


def differ(one, other):
    return (one + other) % 2


def ring_bits(place):
    high = place // 2
    return (place + high) % 2, high


def ring_place(low, high):
    return 2 * high + (low + high) % 2


def blk_bits(index):
    low, high = ring_bits(index % 4)
    return low, high, index // 4


def blk_index(bits):
    return bits[2] * 4 + ring_place(bits[0], bits[1])


def weigh(mine, assign, orders, offsets, row_weight, coupling, right):
    n_rows = right.shape[0]
    n_blocks = assign.shape[0]
    slots = lax.broadcasted_iota(jnp.int32, (1, n_rows), 1)
    members, scaled = [], []
    for block in range(n_blocks):
        start = offsets[block]
        inside = (
            (jnp.full((1, n_rows), assign[block], jnp.int32) == mine)
            & (slots >= start)
            & (slots < start + orders[block])
        ).astype(F32)
        members.append(inside)
        scaled.append(inside / jnp.sqrt(jnp.full((1, n_rows), orders[block], jnp.int32).astype(F32)))
    member = jnp.concatenate(members, axis=0)
    shares = jnp.concatenate(scaled, axis=0)
    right_t = right[...].astype(F32).T
    sums = lax.dot_general(
        right_t * coupling[...], member, (((1,), (1,)), ((), ())), precision=HIGH, preferred_element_type=F32
    )
    spread = lax.dot_general(
        sums, shares, (((1,), (0,)), ((), ())), precision=HIGH, preferred_element_type=F32
    )
    live = jnp.sum(member, axis=0, keepdims=True)
    return (live * row_weight[...] * right_t + coupling[...] * spread).astype(BF16)


def kernel(
    assign, orders, offsets, row_weight, coupling, right, left, out,
    slabs, weights, piece, quarters, partial, arrived, total,
    own_send, own_recv, fwd_send, fwd_recv, sum_send, sum_recv,
    local_sem, part_send, part_recv, z_send, z_recv, zf_send, zf_recv, put_send, put_recv,
    x_send, x_recv, xf_send, xf_recv, core_send, core_recv,
):
    height, width = left.shape
    plan_width = width // PLANS
    step_width = plan_width // STEPS
    half = height // 2
    block = weights.shape[2]
    core_rows = block // 2
    x_rows = core_rows // 4
    blk = lax.axis_index("blk")
    tile = lax.axis_index("tile")
    x, z_hi, core = tile // 4, (tile // 2) % 2, tile % 2
    y, z = blk % 4, z_hi * 2 + blk // 4
    bits = blk_bits(blk)
    x_bits, z_bits = ring_bits(x), ring_bits(z)

    def device(x_to, y_to, z_to, core_to):
        return (z_to % 2) * 4 + y_to, x_to * 4 + (z_to // 2) * 2 + core_to

    def across(dim):
        return blk_index([flip(bit) if at == dim else bit for at, bit in enumerate(bits)]), tile

    def moved(place_bits, *flips):
        return ring_place(*[differ(bit, by) for bit, by in zip(place_bits, flips)])

    x_near = [moved(x_bits, 1, 0), moved(x_bits, 0, 1)]
    x_far = moved(x_bits, 1, 1)
    z_near = [moved(z_bits, 1, 0), moved(z_bits, 0, 1)]
    y_bits = bits[:2]
    x_peers = [device(to, y, z, core) for to in (*x_near, x_far)]
    z_peers = [device(x, y, to, core) for to in z_near]
    y_peers = {by: device(x, moved(y_bits, *by), z, core) for by in ((1, 0), (0, 1), (1, 1))}
    twin = device(x, y, z, 1 - core)

    barrier = pltpu.get_barrier_semaphore()
    peers = [*y_peers.values(), *z_peers, *x_peers, twin]
    for peer in peers:
        pl.semaphore_signal(barrier, inc=1, device_id=peer, device_id_type=MESH)
    pl.semaphore_wait(barrier, len(peers))

    def remote(src, dst, send, recv, peer):
        return pltpu.make_async_remote_copy(
            src_ref=src, dst_ref=dst, send_sem=send, recv_sem=recv,
            device_id=peer, device_id_type=MESH,
        )

    def columns(plan, step):
        return pl.ds(pl.multiple_of(plan * plan_width + step * step_width, step_width), step_width)

    def own_copy(plan, step, side):
        cols = columns(plan, step)
        return remote(
            left.at[:, cols], slabs.at[1 + side, :, cols],
            own_send.at[plan, step, side], own_recv.at[plan, step, side],
            across((plan + 1 + side) % 3),
        )

    def fwd_copy(plan, step, side):
        cols = columns(plan, step)
        rows = pl.ds(side * half, half)
        return remote(
            slabs.at[2 - side, rows, cols], slabs.at[3, rows, cols],
            fwd_send.at[plan, step, side], fwd_recv.at[plan, step, side],
            across((plan + 1 + side) % 3),
        )

    def sum_copy(plan, step):
        cols = columns(plan, step)
        return remote(
            partial.at[:, cols], arrived.at[:, cols],
            sum_send.at[plan, step], sum_recv.at[plan, step], across(plan),
        )

    local = pltpu.make_async_copy(left, slabs.at[0], local_sem.at[0])
    local.start()

    def send_own(step):
        for plan in range(PLANS):
            for side in range(2):
                own_copy(plan, step, side).start()

    send_own(0)

    piece[...] = weigh(blk, assign, orders, offsets, row_weight, coupling, right)

    def quarter(index):
        return piece.at[pl.ds(pl.multiple_of(index * x_rows, x_rows), x_rows), :]

    def part_copy(index):
        place = (*x_near, x_far)[index]
        return remote(
            quarter(place), quarters.at[z, x], part_send.at[index], part_recv.at[index], x_peers[index]
        )

    kept = pltpu.make_async_copy(quarter(x), quarters.at[z, x], local_sem.at[1])
    for index in range(3):
        part_copy(index).start()
    kept.start()

    def z_copy(side):
        return remote(quarters.at[z], quarters.at[z], z_send.at[side], z_recv.at[side], z_peers[side])

    def zf_copy(side):
        part = quarters.at[z_near[1 - side], pl.ds(2 * side, 2)]
        return remote(part, part, zf_send.at[side], zf_recv.at[side], z_peers[side])

    kept.wait()
    for index in range(3):
        part_copy(index).wait_recv()
    for side in range(2):
        z_copy(side).start()

    plane = bits[2]

    def puts(plan):
        for first in range(2):
            for second in range(2):
                if plan < 2:
                    for far in range(2):
                        from_bit, to_bit = first, second
                        own, over = bits[plan], bits[1 - plan]
                        band = [None, None]
                        band[plan], band[1 - plan] = differ(own, from_bit), differ(over, far)
                        slab_plane = to_bit
                        spots = [None, None]
                        spots[plan], spots[1 - plan] = 0, far
                        apart = differ(slab_plane, plane)
                        slot = apart + 2 * far if plan == 1 else far + 2 * apart
                        yield tuple(spots), slab_plane, band, plane, from_bit, slot
                else:
                    for band_plane in range(2):
                        band = [differ(bits[0], first), differ(bits[1], second)]
                        yield (first, second), plane, band, band_plane, differ(band_plane, plane), first + 2 * second

    def x_region(plan, x_from, first, count):
        start = pl.multiple_of(core * core_rows + x_from * x_rows + first, count)
        return weights.at[plan, :, pl.ds(start, count), :]

    def put_copies(plan, with_local):
        for index, (move, slab_plane, band, band_plane, kind, slot) in enumerate(puts(plan)):
            band_z_hi = differ(band[0], band[1])
            band_x = 2 * band_plane + band[1]
            rows = pl.ds(pl.multiple_of(core * core_rows + x * x_rows, x_rows), x_rows)
            lanes = pl.ds(pl.multiple_of(slot * height, height), height)
            src = quarters.at[band_z_hi * 2 + slab_plane, band_x]
            dst = weights.at[plan, kind, rows, lanes]
            if move != (0, 0):
                yield remote(src, dst, put_send.at[plan, index], put_recv.at[plan], y_peers[move])
            elif with_local:
                yield pltpu.make_async_copy(src, dst, put_recv.at[plan])

    def x_copy(plan, side):
        region = x_region(plan, x, 0, x_rows)
        return remote(region, region, x_send.at[plan, side], x_recv.at[plan, side], x_peers[side])

    def xf_copy(plan, side):
        region = x_region(plan, x_near[1 - side], side * (x_rows // 2), x_rows // 2)
        return remote(region, region, xf_send.at[plan, side], xf_recv.at[plan, side], x_peers[side])

    def core_copy(plan, index):
        region = x_region(plan, (x, *x_near, x_far)[index], 0, x_rows)
        return remote(region, region, core_send.at[plan, index], core_recv.at[plan, index], twin)

    def forward(step):
        for plan in range(PLANS):
            for side in range(2):
                own_copy(plan, step, side).wait_recv()
            for side in range(2):
                fwd_copy(plan, step, side).start()

    send_own(1)
    for side in range(2):
        z_copy(side).wait_recv()
    for side in range(2):
        zf_copy(side).start()
    send_own(2)
    forward(0)
    for side in range(2):
        zf_copy(side).wait_recv()
    for plan in range(PLANS):
        for copy in put_copies(plan, True):
            copy.start()
    send_own(3)
    forward(1)
    for plan in range(PLANS):
        region = x_region(plan, x, 0, x_rows)
        pltpu.make_async_copy(region, region, put_recv.at[plan]).wait()
        for side in range(2):
            x_copy(plan, side).start()
        core_copy(plan, 0).start()
    forward(2)
    for plan in range(PLANS):
        for side in range(2):
            x_copy(plan, side).wait_recv()
        for side in range(2):
            xf_copy(plan, side).start()
        for index in (1, 2):
            core_copy(plan, index).start()
    forward(3)
    for plan in range(PLANS):
        for side in range(2):
            xf_copy(plan, side).wait_recv()
        core_copy(plan, 3).start()
    for plan in range(PLANS):
        for index in range(4):
            core_copy(plan, index).wait_recv()
    local.wait()

    def product(plan, kind, cols):
        rows = slabs[:, :, cols].reshape(4 * height, step_width)
        return jnp.dot(weights[plan, kind], rows, preferred_element_type=F32)

    @pl.loop(0, STEPS)
    def _(step):
        for plan in range(PLANS):
            cols = columns(plan, step)
            for side in range(2):
                fwd_copy(plan, step, side).wait_recv()
            partial[:, cols] = product(plan, 1, cols).astype(BF16)
            sum_copy(plan, step).start()
        for plan in range(PLANS):
            cols = columns(plan, step)
            total[:, cols] = product(plan, 0, cols)

    @pl.loop(0, STEPS)
    def _(step):
        for plan in range(PLANS):
            cols = columns(plan, step)
            sum_copy(plan, step).wait_recv()
            out[:, cols] = (total[:, cols] + arrived[:, cols].astype(F32)).astype(BF16)

    for index in range(3):
        part_copy(index).wait_send()
    for side in range(2):
        z_copy(side).wait_send()
        zf_copy(side).wait_send()
    for plan in range(PLANS):
        for copy in put_copies(plan, False):
            copy.wait_send()
        for side in range(2):
            x_copy(plan, side).wait_send()
            xf_copy(plan, side).wait_send()
        for index in range(4):
            core_copy(plan, index).wait_send()

    @pl.loop(0, STEPS)
    def _(step):
        for plan in range(PLANS):
            for side in range(2):
                own_copy(plan, step, side).wait_send()
                fwd_copy(plan, step, side).wait_send()
            sum_copy(plan, step).wait_send()


def shards(left_rows, right_rows, row_weight, coupling, assign, orders, offsets):
    height, width = left_rows.shape
    band = right_rows.shape[1] * lax.axis_size("tile")
    block = band // lax.axis_size("blk")
    dma = pltpu.SemaphoreType.DMA
    smem = pl.BlockSpec(memory_space=pltpu.SMEM)
    vmem = pl.BlockSpec(memory_space=pltpu.VMEM)
    hbm = pl.BlockSpec(memory_space=pl.ANY)
    return pl.pallas_call(
        kernel,
        out_shape=pltpu.VMEM((block, width), BF16),
        in_specs=[smem, smem, smem, vmem, vmem, vmem, hbm],
        out_specs=vmem,
        scratch_shapes=[
            pltpu.VMEM((4, height, width), BF16),
            pltpu.VMEM((PLANS, 2, block, 4 * height), BF16),
            pltpu.VMEM((right_rows.shape[1], height), BF16),
            pltpu.VMEM((4, 4, right_rows.shape[1] // 4, height), BF16),
            pltpu.VMEM((block, width), BF16),
            pltpu.VMEM((block, width), BF16),
            pltpu.VMEM((block, width), F32),
            dma((PLANS, STEPS, 2)), dma((PLANS, STEPS, 2)),
            dma((PLANS, STEPS, 2)), dma((PLANS, STEPS, 2)),
            dma((PLANS, STEPS)), dma((PLANS, STEPS)),
            dma((2,)), dma((3,)), dma((3,)), dma((2,)), dma((2,)), dma((2,)), dma((2,)),
            dma((PLANS, 8)), dma((PLANS,)),
            dma((PLANS, 2)), dma((PLANS, 2)),
            dma((PLANS, 2)), dma((PLANS, 2)),
            dma((PLANS, 4)), dma((PLANS, 4)),
        ],
        compiler_params=pltpu.CompilerParams(collective_id=0, has_side_effects=True, vmem_limit_bytes=60 * 2**20),
    )(
        assign, orders, offsets, row_weight.reshape(1, height), coupling.reshape(1, height), right_rows, left_rows
    )


def solution(mesh):
    return jax.shard_map(
        shards,
        mesh=mesh,
        in_specs=(P("blk", "tile"), P("blk", "tile"), P("blk"), P("blk"), P(), P(), P()),
        out_specs=P("blk", "tile"),
        check_vma=False,
    )
```

time: 93.4 us -> 89.6 us (0.959)
  local copies, waits for them, and re-layouts: 3.76 us -> 1.67 us
  Pallas kernels: 88 us -> 86.3 us
    unnamed x1, local copies, waits for them, and re-layouts: 3.76 us -> 1.67 us
    pallas_call x1, Pallas kernels: 88 us -> 86.3 us  [shards(): pl.pallas_call(kernel, out_shape=pltpu.VMEM((block, width), BF16), in_spe...]
where the time goes in v2:
time: 89.6 us; the launch traced here: 88 us
  Pallas kernels  86.3 us (96%)
  local copies, waits for them, and re-layouts  1.67 us (2%)
    pallas_call x1, Pallas kernels, shards(): pl.pallas_call(kernel, out_shape=pltpu.VMEM((block, width), BF16), in_spe...  86.3 us

profile of v2, /device:TPU:0, one launch (start us, length us, event | category | flops | bytes accessed | tf_op | source)
XLA Modules:
  0.0 88.0 jit_solution(17195506271080717106)
XLA Ops:
  0.0 86.3 %shard_map.73 = bf16[512,3072]{1,0:T(8,128)(2,1)S(1)} custom-call(s32[16]{0:T(128)} %assign.1, s32[16]{0:T(128)} %orders.1, s32[16]{0:T(128)} %offsets.1, f32[1,256]{1,0:T(1,128)} %bitcast.2, f32[1,256]{1,0:T(1,128)} %bitcast.3, bf16[256,256]{1,0:T(8,128)(2,1)} %right.1, bf16[256,3072]{1,0:T(8,128)(2,1)} %left.1), custom_call_target="tpu_custom_call" | custom-call | tf_op jit(solution)/shard_map/pallas_call | solution.py:338
  86.3 1.7 %copy.9 = bf16[512,3072]{1,0:T(8,128)(2,1)} copy(bf16[512,3072]{1,0:T(8,128)(2,1)S(1)} %shard_map.73) | data formatting | bytes 6291456

commit v3 on v2

--- a/solution.py
+++ b/solution.py
@@ -187,32 +187,27 @@
 
     plane = bits[2]
 
-    def puts(plan):
+    def puts(plan, kind):
         for first in range(2):
             for second in range(2):
                 if plan < 2:
-                    for far in range(2):
-                        from_bit, to_bit = first, second
-                        own, over = bits[plan], bits[1 - plan]
-                        band = [None, None]
-                        band[plan], band[1 - plan] = differ(own, from_bit), differ(over, far)
-                        slab_plane = to_bit
-                        spots = [None, None]
-                        spots[plan], spots[1 - plan] = 0, far
-                        apart = differ(slab_plane, plane)
-                        slot = apart + 2 * far if plan == 1 else far + 2 * apart
-                        yield tuple(spots), slab_plane, band, plane, from_bit, slot
+                    far, slab_plane = first, second
+                    band, move = [None, None], [None, None]
+                    band[plan], band[1 - plan] = differ(bits[plan], kind), differ(bits[1 - plan], far)
+                    move[plan], move[1 - plan] = 0, far
+                    apart = differ(slab_plane, plane)
+                    slot = apart + 2 * far if plan == 1 else far + 2 * apart
+                    yield tuple(move), slab_plane, band, plane, kind, slot
                 else:
-                    for band_plane in range(2):
-                        band = [differ(bits[0], first), differ(bits[1], second)]
-                        yield (first, second), plane, band, band_plane, differ(band_plane, plane), first + 2 * second
-
-    def x_region(plan, x_from, first, count):
+                    band = [differ(bits[0], first), differ(bits[1], second)]
+                    yield (first, second), plane, band, differ(plane, kind), kind, first + 2 * second
+
+    def x_region(plan, kind, x_from, first, count):
         start = pl.multiple_of(core * core_rows + x_from * x_rows + first, count)
-        return weights.at[plan, :, pl.ds(start, count), :]
-
-    def put_copies(plan, with_local):
-        for index, (move, slab_plane, band, band_plane, kind, slot) in enumerate(puts(plan)):
+        return weights.at[plan, kind, pl.ds(start, count), :]
+
+    def put_copies(plan, kind_now, with_local):
+        for index, (move, slab_plane, band, band_plane, kind, slot) in enumerate(puts(plan, kind_now)):
             band_z_hi = differ(band[0], band[1])
             band_x = 2 * band_plane + band[1]
             rows = pl.ds(pl.multiple_of(core * core_rows + x * x_rows, x_rows), x_rows)
@@ -220,21 +215,45 @@
             src = quarters.at[band_z_hi * 2 + slab_plane, band_x]
             dst = weights.at[plan, kind, rows, lanes]
             if move != (0, 0):
-                yield remote(src, dst, put_send.at[plan, index], put_recv.at[plan], y_peers[move])
+                yield remote(src, dst, put_send.at[plan, kind, index], put_recv.at[plan, kind], y_peers[move])
             elif with_local:
-                yield pltpu.make_async_copy(src, dst, put_recv.at[plan])
-
-    def x_copy(plan, side):
-        region = x_region(plan, x, 0, x_rows)
-        return remote(region, region, x_send.at[plan, side], x_recv.at[plan, side], x_peers[side])
-
-    def xf_copy(plan, side):
-        region = x_region(plan, x_near[1 - side], side * (x_rows // 2), x_rows // 2)
-        return remote(region, region, xf_send.at[plan, side], xf_recv.at[plan, side], x_peers[side])
-
-    def core_copy(plan, index):
-        region = x_region(plan, (x, *x_near, x_far)[index], 0, x_rows)
-        return remote(region, region, core_send.at[plan, index], core_recv.at[plan, index], twin)
+                yield pltpu.make_async_copy(src, dst, put_recv.at[plan, kind])
+
+    def x_copy(plan, kind, side):
+        region = x_region(plan, kind, x, 0, x_rows)
+        return remote(region, region, x_send.at[plan, kind, side], x_recv.at[plan, kind, side], x_peers[side])
+
+    def xf_copy(plan, kind, side):
+        region = x_region(plan, kind, x_near[1 - side], side * (x_rows // 2), x_rows // 2)
+        return remote(region, region, xf_send.at[plan, kind, side], xf_recv.at[plan, kind, side], x_peers[side])
+
+    def core_copy(plan, kind, index):
+        region = x_region(plan, kind, (x, *x_near, x_far)[index], 0, x_rows)
+        return remote(region, region, core_send.at[plan, kind, index], core_recv.at[plan, kind, index], twin)
+
+    def x_begin(plan, kind):
+        region = x_region(plan, kind, x, 0, x_rows)
+        pltpu.make_async_copy(region, region, put_recv.at[plan, kind]).wait()
+        for side in range(2):
+            x_copy(plan, kind, side).start()
+        core_copy(plan, kind, 0).start()
+
+    def x_pass(plan, kind):
+        for side in range(2):
+            x_copy(plan, kind, side).wait_recv()
+        for side in range(2):
+            xf_copy(plan, kind, side).start()
+        for index in (1, 2):
+            core_copy(plan, kind, index).start()
+
+    def x_end(plan, kind):
+        for side in range(2):
+            xf_copy(plan, kind, side).wait_recv()
+        core_copy(plan, kind, 3).start()
+
+    def core_end(plan, kind):
+        for index in range(4):
+            core_copy(plan, kind, index).wait_recv()
 
     def forward(step):
         for plan in range(PLANS):
@@ -252,33 +271,25 @@
     forward(0)
     for side in range(2):
         zf_copy(side).wait_recv()
-    for plan in range(PLANS):
-        for copy in put_copies(plan, True):
-            copy.start()
-    send_own(3)
-    forward(1)
-    for plan in range(PLANS):
-        region = x_region(plan, x, 0, x_rows)
-        pltpu.make_async_copy(region, region, put_recv.at[plan]).wait()
-        for side in range(2):
-            x_copy(plan, side).start()
-        core_copy(plan, 0).start()
+    for kind in (1, 0):
+        for plan in range(PLANS):
+            for copy in put_copies(plan, kind, True):
+                copy.start()
+        if kind == 1:
+            send_own(3)
+            forward(1)
+    for plan in range(PLANS):
+        x_begin(plan, 1)
     forward(2)
     for plan in range(PLANS):
-        for side in range(2):
-            x_copy(plan, side).wait_recv()
-        for side in range(2):
-            xf_copy(plan, side).start()
-        for index in (1, 2):
-            core_copy(plan, index).start()
+        x_pass(plan, 1)
+    for plan in range(PLANS):
+        x_begin(plan, 0)
     forward(3)
     for plan in range(PLANS):
-        for side in range(2):
-            xf_copy(plan, side).wait_recv()
-        core_copy(plan, 3).start()
-    for plan in range(PLANS):
-        for index in range(4):
-            core_copy(plan, index).wait_recv()
+        x_end(plan, 1)
+    for plan in range(PLANS):
+        core_end(plan, 1)
     local.wait()
 
     def product(plan, kind, cols):
@@ -293,6 +304,13 @@
                 fwd_copy(plan, step, side).wait_recv()
             partial[:, cols] = product(plan, 1, cols).astype(BF16)
             sum_copy(plan, step).start()
+
+    for stage in (x_pass, x_end, core_end):
+        for plan in range(PLANS):
+            stage(plan, 0)
+
+    @pl.loop(0, STEPS)
+    def _(step):
         for plan in range(PLANS):
             cols = columns(plan, step)
             total[:, cols] = product(plan, 0, cols)
@@ -310,13 +328,14 @@
         z_copy(side).wait_send()
         zf_copy(side).wait_send()
     for plan in range(PLANS):
-        for copy in put_copies(plan, False):
-            copy.wait_send()
-        for side in range(2):
-            x_copy(plan, side).wait_send()
-            xf_copy(plan, side).wait_send()
-        for index in range(4):
-            core_copy(plan, index).wait_send()
+        for kind in range(2):
+            for copy in put_copies(plan, kind, False):
+                copy.wait_send()
+            for side in range(2):
+                x_copy(plan, kind, side).wait_send()
+                xf_copy(plan, kind, side).wait_send()
+            for index in range(4):
+                core_copy(plan, kind, index).wait_send()
 
     @pl.loop(0, STEPS)
     def _(step):
@@ -352,10 +371,10 @@
             dma((PLANS, STEPS, 2)), dma((PLANS, STEPS, 2)),
             dma((PLANS, STEPS)), dma((PLANS, STEPS)),
             dma((2,)), dma((3,)), dma((3,)), dma((2,)), dma((2,)), dma((2,)), dma((2,)),
-            dma((PLANS, 8)), dma((PLANS,)),
-            dma((PLANS, 2)), dma((PLANS, 2)),
-            dma((PLANS, 2)), dma((PLANS, 2)),
-            dma((PLANS, 4)), dma((PLANS, 4)),
+            dma((PLANS, 2, 4)), dma((PLANS, 2)),
+            dma((PLANS, 2, 2)), dma((PLANS, 2, 2)),
+            dma((PLANS, 2, 2)), dma((PLANS, 2, 2)),
+            dma((PLANS, 2, 4)), dma((PLANS, 2, 4)),
         ],
         compiler_params=pltpu.CompilerParams(collective_id=0, has_side_effects=True, vmem_limit_bytes=60 * 2**20),
     )(

time: 89.6 us -> 78.1 us (0.87)
  Pallas kernels: 86.3 us -> 75 us
    pallas_call x1, Pallas kernels: 86.3 us -> 75 us  [shards(): pl.pallas_call(kernel, out_shape=pltpu.VMEM((block, width), BF16), in_spe...]
where the time goes in v3:
time: 78.1 us; the launch traced here: 76.6 us
  Pallas kernels  75 us (96%)
  local copies, waits for them, and re-layouts  1.67 us (2%)
    pallas_call x1, Pallas kernels, shards(): pl.pallas_call(kernel, out_shape=pltpu.VMEM((block, width), BF16), in_spe...  75 us
    unnamed x1, local copies, waits for them, and re-layouts  1.67 us

profile of v3, /device:TPU:0, one launch (start us, length us, event | category | flops | bytes accessed | tf_op | source)
XLA Modules:
  0.0 76.6 jit_solution(14451231693480990525)
XLA Ops:
  0.0 75.0 %shard_map.73 = bf16[512,3072]{1,0:T(8,128)(2,1)S(1)} custom-call(s32[16]{0:T(128)} %assign.1, s32[16]{0:T(128)} %orders.1, s32[16]{0:T(128)} %offsets.1, f32[1,256]{1,0:T(1,128)} %bitcast.2, f32[1,256]{1,0:T(1,128)} %bitcast.3, bf16[256,256]{1,0:T(8,128)(2,1)} %right.1, bf16[256,3072]{1,0:T(8,128)(2,1)} %left.1), custom_call_target="tpu_custom_call" | custom-call | tf_op jit(solution)/shard_map/pallas_call | solution.py:357
  75.0 1.7 %copy.9 = bf16[512,3072]{1,0:T(8,128)(2,1)} copy(bf16[512,3072]{1,0:T(8,128)(2,1)S(1)} %shard_map.73) | data formatting | bytes 6291456

commit v4 on v3

--- a/solution.py
+++ b/solution.py
@@ -12,6 +12,7 @@
 BF16 = jnp.bfloat16
 HIGH = lax.Precision.HIGHEST
 PLANS = 3
+OWN = 3
 STEPS = 4
 
 
@@ -70,7 +71,7 @@
 
 def kernel(
     assign, orders, offsets, row_weight, coupling, right, left, out,
-    slabs, weights, piece, quarters, partial, arrived, total,
+    slabs, weights, own_weights, piece, quarters, partial, arrived, total,
     own_send, own_recv, fwd_send, fwd_recv, sum_send, sum_recv,
     local_sem, part_send, part_recv, z_send, z_recv, zf_send, zf_recv, put_send, put_recv,
     x_send, x_recv, xf_send, xf_recv, core_send, core_recv,
@@ -79,7 +80,7 @@
     plan_width = width // PLANS
     step_width = plan_width // STEPS
     half = height // 2
-    block = weights.shape[2]
+    block = weights.shape[1]
     core_rows = block // 2
     x_rows = core_rows // 4
     blk = lax.axis_index("blk")
@@ -111,6 +112,9 @@
     peers = [*y_peers.values(), *z_peers, *x_peers, twin]
     for peer in peers:
         pl.semaphore_signal(barrier, inc=1, device_id=peer, device_id_type=MESH)
+    local = pltpu.make_async_copy(left, slabs.at[0], local_sem.at[0])
+    local.start()
+    piece[...] = weigh(blk, assign, orders, offsets, row_weight, coupling, right)
     pl.semaphore_wait(barrier, len(peers))
 
     def remote(src, dst, send, recv, peer):
@@ -146,17 +150,13 @@
             sum_send.at[plan, step], sum_recv.at[plan, step], across(plan),
         )
 
-    local = pltpu.make_async_copy(left, slabs.at[0], local_sem.at[0])
-    local.start()
-
-    def send_own(step):
-        for plan in range(PLANS):
-            for side in range(2):
-                own_copy(plan, step, side).start()
-
-    send_own(0)
-
-    piece[...] = weigh(blk, assign, orders, offsets, row_weight, coupling, right)
+    def send_own(step, *sent):
+        for plan, side in sent:
+            own_copy(plan, step, side).start()
+
+    over_y = ((0, 0), (1, 1), (2, 0), (2, 1))
+    send_own(0, *over_y, (0, 1))
+
 
     def quarter(index):
         return piece.at[pl.ds(pl.multiple_of(index * x_rows, x_rows), x_rows), :]
@@ -187,73 +187,82 @@
 
     plane = bits[2]
 
-    def puts(plan, kind):
+    def puts(unit):
+        if unit == OWN:
+            for slot in range(7):
+                move = (slot % 2, slot // 2 % 2)
+                band = [differ(bits[0], move[0]), differ(bits[1], move[1])]
+                yield move, differ(plane, slot // 4), band, plane, slot
+            return
         for first in range(2):
             for second in range(2):
-                if plan < 2:
+                if unit < 2:
                     far, slab_plane = first, second
                     band, move = [None, None], [None, None]
-                    band[plan], band[1 - plan] = differ(bits[plan], kind), differ(bits[1 - plan], far)
-                    move[plan], move[1 - plan] = 0, far
+                    band[unit], band[1 - unit] = flip(bits[unit]), differ(bits[1 - unit], far)
+                    move[unit], move[1 - unit] = 0, far
                     apart = differ(slab_plane, plane)
-                    slot = apart + 2 * far if plan == 1 else far + 2 * apart
-                    yield tuple(move), slab_plane, band, plane, kind, slot
+                    yield tuple(move), slab_plane, band, plane, apart + 2 * far if unit == 1 else far + 2 * apart
                 else:
                     band = [differ(bits[0], first), differ(bits[1], second)]
-                    yield (first, second), plane, band, differ(plane, kind), kind, first + 2 * second
-
-    def x_region(plan, kind, x_from, first, count):
+                    yield (first, second), plane, band, flip(plane), first + 2 * second
+
+    def store(unit):
+        return own_weights if unit == OWN else weights.at[unit]
+
+    def x_region(unit, x_from, first, count):
         start = pl.multiple_of(core * core_rows + x_from * x_rows + first, count)
-        return weights.at[plan, kind, pl.ds(start, count), :]
-
-    def put_copies(plan, kind_now, with_local):
-        for index, (move, slab_plane, band, band_plane, kind, slot) in enumerate(puts(plan, kind_now)):
+        rows = pl.ds(start, count)
+        return own_weights.at[rows, pl.ds(0, 7 * height)] if unit == OWN else weights.at[unit, rows, :]
+
+    def put_copies(unit, with_local):
+        for index, (move, slab_plane, band, band_plane, slot) in enumerate(puts(unit)):
             band_z_hi = differ(band[0], band[1])
             band_x = 2 * band_plane + band[1]
             rows = pl.ds(pl.multiple_of(core * core_rows + x * x_rows, x_rows), x_rows)
             lanes = pl.ds(pl.multiple_of(slot * height, height), height)
             src = quarters.at[band_z_hi * 2 + slab_plane, band_x]
-            dst = weights.at[plan, kind, rows, lanes]
+            dst = store(unit).at[rows, lanes]
             if move != (0, 0):
-                yield remote(src, dst, put_send.at[plan, kind, index], put_recv.at[plan, kind], y_peers[move])
+                yield remote(src, dst, put_send.at[unit, index], put_recv.at[unit], y_peers[move])
             elif with_local:
-                yield pltpu.make_async_copy(src, dst, put_recv.at[plan, kind])
-
-    def x_copy(plan, kind, side):
-        region = x_region(plan, kind, x, 0, x_rows)
-        return remote(region, region, x_send.at[plan, kind, side], x_recv.at[plan, kind, side], x_peers[side])
-
-    def xf_copy(plan, kind, side):
-        region = x_region(plan, kind, x_near[1 - side], side * (x_rows // 2), x_rows // 2)
-        return remote(region, region, xf_send.at[plan, kind, side], xf_recv.at[plan, kind, side], x_peers[side])
-
-    def core_copy(plan, kind, index):
-        region = x_region(plan, kind, (x, *x_near, x_far)[index], 0, x_rows)
-        return remote(region, region, core_send.at[plan, kind, index], core_recv.at[plan, kind, index], twin)
-
-    def x_begin(plan, kind):
-        region = x_region(plan, kind, x, 0, x_rows)
-        pltpu.make_async_copy(region, region, put_recv.at[plan, kind]).wait()
+                yield pltpu.make_async_copy(src, dst, put_recv.at[unit])
+
+    def x_copy(unit, side):
+        region = x_region(unit, x, 0, x_rows)
+        return remote(region, region, x_send.at[unit, side], x_recv.at[unit, side], x_peers[side])
+
+    def xf_copy(unit, side):
+        region = x_region(unit, x_near[1 - side], side * (x_rows // 2), x_rows // 2)
+        return remote(region, region, xf_send.at[unit, side], xf_recv.at[unit, side], x_peers[side])
+
+    def core_copy(unit, index):
+        region = x_region(unit, (x, *x_near, x_far)[index], 0, x_rows)
+        return remote(region, region, core_send.at[unit, index], core_recv.at[unit, index], twin)
+
+    def x_begin(unit):
+        region = x_region(unit, x, 0, x_rows)
+        pltpu.make_async_copy(region, region, put_recv.at[unit]).wait()
         for side in range(2):
-            x_copy(plan, kind, side).start()
-        core_copy(plan, kind, 0).start()
-
-    def x_pass(plan, kind):
+            x_copy(unit, side).start()
+        core_copy(unit, 0).start()
+
+    def x_pass(unit):
         for side in range(2):
-            x_copy(plan, kind, side).wait_recv()
+            x_copy(unit, side).wait_recv()
         for side in range(2):
-            xf_copy(plan, kind, side).start()
+            xf_copy(unit, side).start()
         for index in (1, 2):
-            core_copy(plan, kind, index).start()
-
-    def x_end(plan, kind):
+            core_copy(unit, index).start()
+
+    def x_end(unit):
         for side in range(2):
-            xf_copy(plan, kind, side).wait_recv()
-        core_copy(plan, kind, 3).start()
-
-    def core_end(plan, kind):
+            xf_copy(unit, side).wait_recv()
+        core_copy(unit, 3).start()
+
+    def core_end(unit):
         for index in range(4):
-            core_copy(plan, kind, index).wait_recv()
+            core_copy(unit, index).wait_recv()
 
     def forward(step):
         for plan in range(PLANS):
@@ -262,39 +271,50 @@
             for side in range(2):
                 fwd_copy(plan, step, side).start()
 
-    send_own(1)
+    send_own(0, (1, 0))
+    send_own(1, *over_y)
     for side in range(2):
         z_copy(side).wait_recv()
     for side in range(2):
         zf_copy(side).start()
-    send_own(2)
-    forward(0)
+    send_own(1, (0, 1), (1, 0))
+    send_own(2, (2, 0), (2, 1))
     for side in range(2):
         zf_copy(side).wait_recv()
-    for kind in (1, 0):
-        for plan in range(PLANS):
-            for copy in put_copies(plan, kind, True):
-                copy.start()
-        if kind == 1:
-            send_own(3)
-            forward(1)
-    for plan in range(PLANS):
-        x_begin(plan, 1)
+    for unit in range(PLANS):
+        for copy in put_copies(unit, True):
+            copy.start()
+    send_own(2, (0, 0), (1, 1), (0, 1), (1, 0))
+    forward(0)
+    for unit in range(PLANS):
+        x_begin(unit)
+    send_own(3, *over_y, (0, 1), (1, 0))
+    forward(1)
+    for unit in range(PLANS):
+        x_pass(unit)
+    for copy in put_copies(OWN, True):
+        copy.start()
     forward(2)
-    for plan in range(PLANS):
-        x_pass(plan, 1)
-    for plan in range(PLANS):
-        x_begin(plan, 0)
+    for unit in range(PLANS):
+        x_end(unit)
+    for unit in range(PLANS):
+        core_end(unit)
     forward(3)
-    for plan in range(PLANS):
-        x_end(plan, 1)
-    for plan in range(PLANS):
-        core_end(plan, 1)
+    x_begin(OWN)
     local.wait()
 
-    def product(plan, kind, cols):
+    def partner_product(plan, cols):
         rows = slabs[:, :, cols].reshape(4 * height, step_width)
-        return jnp.dot(weights[plan, kind], rows, preferred_element_type=F32)
+        return jnp.dot(weights[plan], rows, preferred_element_type=F32)
+
+    def own_product(plan, cols):
+        result = None
+        for slot in range(4):
+            apart = (slot % 2) * 2 ** ((plan + 1) % 3) + (slot // 2) * 2 ** ((plan + 2) % 3)
+            lanes = pl.ds(apart * height, height)
+            term = jnp.dot(own_weights[:, lanes], slabs[slot, :, cols], preferred_element_type=F32)
+            result = term if result is None else result + term
+        return result
 
     @pl.loop(0, STEPS)
     def _(step):
@@ -302,18 +322,17 @@
             cols = columns(plan, step)
             for side in range(2):
                 fwd_copy(plan, step, side).wait_recv()
-            partial[:, cols] = product(plan, 1, cols).astype(BF16)
+            partial[:, cols] = partner_product(plan, cols).astype(BF16)
             sum_copy(plan, step).start()
 
     for stage in (x_pass, x_end, core_end):
-        for plan in range(PLANS):
-            stage(plan, 0)
+        stage(OWN)
 
     @pl.loop(0, STEPS)
     def _(step):
         for plan in range(PLANS):
             cols = columns(plan, step)
-            total[:, cols] = product(plan, 0, cols)
+            total[:, cols] = own_product(plan, cols)
 
     @pl.loop(0, STEPS)
     def _(step):
@@ -327,15 +346,14 @@
     for side in range(2):
         z_copy(side).wait_send()
         zf_copy(side).wait_send()
-    for plan in range(PLANS):
-        for kind in range(2):
-            for copy in put_copies(plan, kind, False):
-                copy.wait_send()
-            for side in range(2):
-                x_copy(plan, kind, side).wait_send()
-                xf_copy(plan, kind, side).wait_send()
-            for index in range(4):
-                core_copy(plan, kind, index).wait_send()
+    for unit in range(PLANS + 1):
+        for copy in put_copies(unit, False):
+            copy.wait_send()
+        for side in range(2):
+            x_copy(unit, side).wait_send()
+            xf_copy(unit, side).wait_send()
+        for index in range(4):
+            core_copy(unit, index).wait_send()
 
     @pl.loop(0, STEPS)
     def _(step):
@@ -361,7 +379,8 @@
         out_specs=vmem,
         scratch_shapes=[
             pltpu.VMEM((4, height, width), BF16),
-            pltpu.VMEM((PLANS, 2, block, 4 * height), BF16),
+            pltpu.VMEM((PLANS, block, 4 * height), BF16),
+            pltpu.VMEM((block, 8 * height), BF16),
             pltpu.VMEM((right_rows.shape[1], height), BF16),
             pltpu.VMEM((4, 4, right_rows.shape[1] // 4, height), BF16),
             pltpu.VMEM((block, width), BF16),
@@ -371,10 +390,10 @@
             dma((PLANS, STEPS, 2)), dma((PLANS, STEPS, 2)),
             dma((PLANS, STEPS)), dma((PLANS, STEPS)),
             dma((2,)), dma((3,)), dma((3,)), dma((2,)), dma((2,)), dma((2,)), dma((2,)),
-            dma((PLANS, 2, 4)), dma((PLANS, 2)),
-            dma((PLANS, 2, 2)), dma((PLANS, 2, 2)),
-            dma((PLANS, 2, 2)), dma((PLANS, 2, 2)),
-            dma((PLANS, 2, 4)), dma((PLANS, 2, 4)),
+            dma((PLANS + 1, 7)), dma((PLANS + 1,)),
+            dma((PLANS + 1, 2)), dma((PLANS + 1, 2)),
+            dma((PLANS + 1, 2)), dma((PLANS + 1, 2)),
+            dma((PLANS + 1, 4)), dma((PLANS + 1, 4)),
         ],
         compiler_params=pltpu.CompilerParams(collective_id=0, has_side_effects=True, vmem_limit_bytes=60 * 2**20),
     )(

time: 78.1 us -> 74.2 us (0.950); the launches traced: 76.6 us -> 74.1 us
  Pallas kernels: 75 us -> 72.4 us
    pallas_call x1, Pallas kernels: 75 us -> 72.4 us  [shards(): pl.pallas_call(kernel, out_shape=pltpu.VMEM((block, width), BF16), in_spe...]
where the time goes in v4:
time: 74.2 us; the launch traced here: 74.1 us
  Pallas kernels  72.4 us (98%)
  local copies, waits for them, and re-layouts  1.67 us (2%)
    pallas_call x1, Pallas kernels, shards(): pl.pallas_call(kernel, out_shape=pltpu.VMEM((block, width), BF16), in_spe...  72.4 us
    unnamed x1, local copies, waits for them, and re-layouts  1.67 us

profile of v4, /device:TPU:0, one launch (start us, length us, event | category | flops | bytes accessed | tf_op | source)
XLA Modules:
  0.0 74.1 jit_solution(15997863577907907595)
XLA Ops:
  0.0 72.4 %shard_map.73 = bf16[512,3072]{1,0:T(8,128)(2,1)S(1)} custom-call(s32[16]{0:T(128)} %assign.1, s32[16]{0:T(128)} %orders.1, s32[16]{0:T(128)} %offsets.1, f32[1,256]{1,0:T(1,128)} %bitcast.2, f32[1,256]{1,0:T(1,128)} %bitcast.3, bf16[256,256]{1,0:T(8,128)(2,1)} %right.1, bf16[256,3072]{1,0:T(8,128)(2,1)} %left.1), custom_call_target="tpu_custom_call" | custom-call | tf_op jit(solution)/shard_map/pallas_call | solution.py:375
  72.4 1.7 %copy.9 = bf16[512,3072]{1,0:T(8,128)(2,1)} copy(bf16[512,3072]{1,0:T(8,128)(2,1)S(1)} %shard_map.73) | data formatting | bytes 6291456

commit v5 on v4

--- a/solution.py
+++ b/solution.py
@@ -70,10 +70,11 @@
 
 
 def kernel(
-    assign, orders, offsets, row_weight, coupling, right, left, out,
+    assign_in, orders_in, offsets_in, row_weight_in, coupling_in, right_in, left, out,
+    assign, orders, offsets, row_weight, coupling, right,
     slabs, weights, own_weights, piece, quarters, partial, arrived, total,
     own_send, own_recv, fwd_send, fwd_recv, sum_send, sum_recv,
-    local_sem, part_send, part_recv, z_send, z_recv, zf_send, zf_recv, put_send, put_recv,
+    small_sem, local_sem, part_send, part_recv, z_send, z_recv, zf_send, zf_recv, put_send, put_recv,
     x_send, x_recv, xf_send, xf_recv, core_send, core_recv,
 ):
     height, width = left.shape
@@ -114,6 +115,13 @@
         pl.semaphore_signal(barrier, inc=1, device_id=peer, device_id_type=MESH)
     local = pltpu.make_async_copy(left, slabs.at[0], local_sem.at[0])
     local.start()
+    small = ((assign_in, assign), (orders_in, orders), (offsets_in, offsets),
+             (row_weight_in, row_weight), (coupling_in, coupling), (right_in, right))
+    fetches = [pltpu.make_async_copy(src, dst, small_sem.at[at]) for at, (src, dst) in enumerate(small)]
+    for fetch in fetches:
+        fetch.start()
+    for fetch in fetches:
+        fetch.wait()
     piece[...] = weigh(blk, assign, orders, offsets, row_weight, coupling, right)
     pl.semaphore_wait(barrier, len(peers))
 
@@ -334,13 +342,6 @@
             cols = columns(plan, step)
             total[:, cols] = own_product(plan, cols)
 
-    @pl.loop(0, STEPS)
-    def _(step):
-        for plan in range(PLANS):
-            cols = columns(plan, step)
-            sum_copy(plan, step).wait_recv()
-            out[:, cols] = (total[:, cols] + arrived[:, cols].astype(F32)).astype(BF16)
-
     for index in range(3):
         part_copy(index).wait_send()
     for side in range(2):
@@ -361,6 +362,13 @@
             for side in range(2):
                 own_copy(plan, step, side).wait_send()
                 fwd_copy(plan, step, side).wait_send()
+
+    @pl.loop(0, STEPS)
+    def _(step):
+        for plan in range(PLANS):
+            cols = columns(plan, step)
+            sum_copy(plan, step).wait_recv()
+            out[:, cols] = (total[:, cols] + arrived[:, cols].astype(F32)).astype(BF16)
             sum_copy(plan, step).wait_send()
 
 
@@ -369,15 +377,16 @@
     band = right_rows.shape[1] * lax.axis_size("tile")
     block = band // lax.axis_size("blk")
     dma = pltpu.SemaphoreType.DMA
-    smem = pl.BlockSpec(memory_space=pltpu.SMEM)
     vmem = pl.BlockSpec(memory_space=pltpu.VMEM)
     hbm = pl.BlockSpec(memory_space=pl.ANY)
     return pl.pallas_call(
         kernel,
         out_shape=pltpu.VMEM((block, width), BF16),
-        in_specs=[smem, smem, smem, vmem, vmem, vmem, hbm],
+        in_specs=[hbm] * 7,
         out_specs=vmem,
         scratch_shapes=[
+            *[pltpu.SMEM(assign.shape, jnp.int32)] * 3,
+            pltpu.VMEM((1, height), F32), pltpu.VMEM((1, height), F32), pltpu.VMEM(right_rows.shape, BF16),
             pltpu.VMEM((4, height, width), BF16),
             pltpu.VMEM((PLANS, block, 4 * height), BF16),
             pltpu.VMEM((block, 8 * height), BF16),
@@ -389,7 +398,7 @@
             dma((PLANS, STEPS, 2)), dma((PLANS, STEPS, 2)),
             dma((PLANS, STEPS, 2)), dma((PLANS, STEPS, 2)),
             dma((PLANS, STEPS)), dma((PLANS, STEPS)),
-            dma((2,)), dma((3,)), dma((3,)), dma((2,)), dma((2,)), dma((2,)), dma((2,)),
+            dma((6,)), dma((2,)), dma((3,)), dma((3,)), dma((2,)), dma((2,)), dma((2,)), dma((2,)),
             dma((PLANS + 1, 7)), dma((PLANS + 1,)),
             dma((PLANS + 1, 2)), dma((PLANS + 1, 2)),
             dma((PLANS + 1, 2)), dma((PLANS + 1, 2)),

time: 74.2 us -> 73 us (0.984)
  Pallas kernels: 72.4 us -> 71.2 us
    pallas_call x1, Pallas kernels: 72.4 us -> 71.2 us  [shards(): pl.pallas_call(kernel, out_shape=pltpu.VMEM((block, width), BF16), in_spe...]
where the time goes in v5:
time: 73 us; the launch traced here: 72.8 us
  Pallas kernels  71.2 us (98%)
  local copies, waits for them, and re-layouts  1.67 us (2%)
    pallas_call x1, Pallas kernels, shards(): pl.pallas_call(kernel, out_shape=pltpu.VMEM((block, width), BF16), in_spe...  71.2 us
    unnamed x1, local copies, waits for them, and re-layouts  1.67 us

profile of v5, /device:TPU:0, one launch (start us, length us, event | category | flops | bytes accessed | tf_op | source)
XLA Modules:
  0.0 72.8 jit_solution(11339277050329055057)
XLA Ops:
  0.0 71.2 %shard_map.73 = bf16[512,3072]{1,0:T(8,128)(2,1)S(1)} custom-call(s32[16]{0:T(128)} %assign_in.1, s32[16]{0:T(128)} %orders_in.1, s32[16]{0:T(128)} %offsets_in.1, f32[1,256]{1,0:T(1,128)} %bitcast.2, f32[1,256]{1,0:T(1,128)} %bitcast.3, bf16[256,256]{1,0:T(8,128)(2,1)} %right_in.1, bf16[256,3072]{1,0:T(8,128)(2,1)} %left.1), custom_call_target="tpu_custom_call" | custom-call | tf_op jit(solution)/shard_map/pallas_call | solution.py:382
  71.2 1.7 %copy.9 = bf16[512,3072]{1,0:T(8,128)(2,1)} copy(bf16[512,3072]{1,0:T(8,128)(2,1)S(1)} %shard_map.73) | data formatting | bytes 6291456

commit v6 on v5

--- a/solution.py
+++ b/solution.py
@@ -13,6 +13,7 @@
 HIGH = lax.Precision.HIGHEST
 PLANS = 3
 OWN = 3
+FORWARD_ROWS = ((112, 144), (144, 112), (128, 128))
 STEPS = 4
 
 
@@ -80,7 +81,6 @@
     height, width = left.shape
     plan_width = width // PLANS
     step_width = plan_width // STEPS
-    half = height // 2
     block = weights.shape[1]
     core_rows = block // 2
     x_rows = core_rows // 4
@@ -144,18 +144,20 @@
 
     def fwd_copy(plan, step, side):
         cols = columns(plan, step)
-        rows = pl.ds(side * half, half)
+        shares = FORWARD_ROWS[plan]
+        rows = pl.ds(side * shares[0], shares[side])
         return remote(
             slabs.at[2 - side, rows, cols], slabs.at[3, rows, cols],
             fwd_send.at[plan, step, side], fwd_recv.at[plan, step, side],
             across((plan + 1 + side) % 3),
         )
 
-    def sum_copy(plan, step):
+    def sum_copy(plan, step, part):
         cols = columns(plan, step)
+        rows = pl.ds(part * core_rows, core_rows)
         return remote(
-            partial.at[:, cols], arrived.at[:, cols],
-            sum_send.at[plan, step], sum_recv.at[plan, step], across(plan),
+            partial.at[rows, cols], arrived.at[rows, cols],
+            sum_send.at[plan, step, part], sum_recv.at[plan, step, part], across(plan),
         )
 
     def send_own(step, *sent):
@@ -180,20 +182,27 @@
         part_copy(index).start()
     kept.start()
 
-    def z_copy(side):
-        return remote(quarters.at[z], quarters.at[z], z_send.at[side], z_recv.at[side], z_peers[side])
-
-    def zf_copy(side):
-        part = quarters.at[z_near[1 - side], pl.ds(2 * side, 2)]
-        return remote(part, part, zf_send.at[side], zf_recv.at[side], z_peers[side])
+    plane = bits[2]
+
+    def z_copies(side):
+        for at, part in enumerate((pl.ds(2 * flip(plane), 2), pl.ds(2 * plane + side, 1))):
+            region = quarters.at[z, part]
+            yield remote(region, region, z_send.at[side, at], z_recv.at[side, at], z_peers[side])
+
+    def zf_copies(side):
+        for at, place in enumerate((plane, flip(plane))):
+            region = quarters.at[z_near[1 - side], 2 * place + 1 - side]
+            yield remote(region, region, zf_send.at[side, at], zf_recv.at[side, at], z_peers[side])
+
+    def each(copies, act):
+        for side in range(2):
+            for copy in copies(side):
+                getattr(copy, act)()
 
     kept.wait()
     for index in range(3):
         part_copy(index).wait_recv()
-    for side in range(2):
-        z_copy(side).start()
-
-    plane = bits[2]
+    each(z_copies, "start")
 
     def puts(unit):
         if unit == OWN:
@@ -281,14 +290,11 @@
 
     send_own(0, (1, 0))
     send_own(1, *over_y)
-    for side in range(2):
-        z_copy(side).wait_recv()
-    for side in range(2):
-        zf_copy(side).start()
+    each(z_copies, "wait_recv")
+    each(zf_copies, "start")
     send_own(1, (0, 1), (1, 0))
     send_own(2, (2, 0), (2, 1))
-    for side in range(2):
-        zf_copy(side).wait_recv()
+    each(zf_copies, "wait_recv")
     for unit in range(PLANS):
         for copy in put_copies(unit, True):
             copy.start()
@@ -300,14 +306,14 @@
     forward(1)
     for unit in range(PLANS):
         x_pass(unit)
+    forward(2)
     for copy in put_copies(OWN, True):
         copy.start()
-    forward(2)
     for unit in range(PLANS):
         x_end(unit)
+    forward(3)
     for unit in range(PLANS):
         core_end(unit)
-    forward(3)
     x_begin(OWN)
     local.wait()
 
@@ -331,7 +337,8 @@
             for side in range(2):
                 fwd_copy(plan, step, side).wait_recv()
             partial[:, cols] = partner_product(plan, cols).astype(BF16)
-            sum_copy(plan, step).start()
+            for part in range(2):
+                sum_copy(plan, step, part).start()
 
     for stage in (x_pass, x_end, core_end):
         stage(OWN)
@@ -344,9 +351,8 @@
 
     for index in range(3):
         part_copy(index).wait_send()
-    for side in range(2):
-        z_copy(side).wait_send()
-        zf_copy(side).wait_send()
+    each(z_copies, "wait_send")
+    each(zf_copies, "wait_send")
     for unit in range(PLANS + 1):
         for copy in put_copies(unit, False):
             copy.wait_send()
@@ -365,11 +371,12 @@
 
     @pl.loop(0, STEPS)
     def _(step):
-        for plan in range(PLANS):
-            cols = columns(plan, step)
-            sum_copy(plan, step).wait_recv()
-            out[:, cols] = (total[:, cols] + arrived[:, cols].astype(F32)).astype(BF16)
-            sum_copy(plan, step).wait_send()
+        for part in range(2):
+            rows = pl.ds(part * core_rows, core_rows)
+            for plan in range(PLANS):
+                cols = columns(plan, step)
+                sum_copy(plan, step, part).wait()
+                out[rows, cols] = (total[rows, cols] + arrived[rows, cols].astype(F32)).astype(BF16)
 
 
 def shards(left_rows, right_rows, row_weight, coupling, assign, orders, offsets):
@@ -397,8 +404,8 @@
             pltpu.VMEM((block, width), F32),
             dma((PLANS, STEPS, 2)), dma((PLANS, STEPS, 2)),
             dma((PLANS, STEPS, 2)), dma((PLANS, STEPS, 2)),
-            dma((PLANS, STEPS)), dma((PLANS, STEPS)),
-            dma((6,)), dma((2,)), dma((3,)), dma((3,)), dma((2,)), dma((2,)), dma((2,)), dma((2,)),
+            dma((PLANS, STEPS, 2)), dma((PLANS, STEPS, 2)),
+            dma((6,)), dma((2,)), dma((3,)), dma((3,)), dma((2, 2)), dma((2, 2)), dma((2, 2)), dma((2, 2)),
             dma((PLANS + 1, 7)), dma((PLANS + 1,)),
             dma((PLANS + 1, 2)), dma((PLANS + 1, 2)),
             dma((PLANS + 1, 2)), dma((PLANS + 1, 2)),

time: 73 us -> 72.6 us (level)
  no operation moved by 1% of the time
where the time goes in v6:
time: 72.6 us; the launch traced here: 72.4 us
  Pallas kernels  70.8 us (98%)
  local copies, waits for them, and re-layouts  1.67 us (2%)
    pallas_call x1, Pallas kernels, shards(): pl.pallas_call(kernel, out_shape=pltpu.VMEM((block, width), BF16), in_spe...  70.8 us
    unnamed x1, local copies, waits for them, and re-layouts  1.67 us

profile of v6, /device:TPU:0, one launch (start us, length us, event | category | flops | bytes accessed | tf_op | source)
XLA Modules:
  0.0 72.4 jit_solution(13651812257221162544)
XLA Ops:
  0.0 70.8 %shard_map.73 = bf16[512,3072]{1,0:T(8,128)(2,1)S(1)} custom-call(s32[16]{0:T(128)} %assign_in.1, s32[16]{0:T(128)} %orders_in.1, s32[16]{0:T(128)} %offsets_in.1, f32[1,256]{1,0:T(1,128)} %bitcast.2, f32[1,256]{1,0:T(1,128)} %bitcast.3, bf16[256,256]{1,0:T(8,128)(2,1)} %right_in.1, bf16[256,3072]{1,0:T(8,128)(2,1)} %left.1), custom_call_target="tpu_custom_call" | custom-call | tf_op jit(solution)/shard_map/pallas_call | solution.py:389
  70.8 1.7 %copy.9 = bf16[512,3072]{1,0:T(8,128)(2,1)} copy(bf16[512,3072]{1,0:T(8,128)(2,1)S(1)} %shard_map.73) | data formatting | bytes 6291456

commit v7 on v6

--- a/solution.py
+++ b/solution.py
@@ -13,6 +13,7 @@
 HIGH = lax.Precision.HIGHEST
 PLANS = 3
 OWN = 3
+SHIFTED = 3
 FORWARD_ROWS = ((112, 144), (144, 112), (128, 128))
 STEPS = 4
 
@@ -75,7 +76,7 @@
     assign, orders, offsets, row_weight, coupling, right,
     slabs, weights, own_weights, piece, quarters, partial, arrived, total,
     own_send, own_recv, fwd_send, fwd_recv, sum_send, sum_recv,
-    small_sem, local_sem, part_send, part_recv, z_send, z_recv, zf_send, zf_recv, put_send, put_recv,
+    small_sem, local_sem, part_send, part_recv, z_send, z_recv, zf_send, zf_recv, put_send, put_recv, chain_send,
     x_send, x_recv, xf_send, xf_recv, core_send, core_recv,
 ):
     height, width = left.shape
@@ -144,7 +145,7 @@
 
     def fwd_copy(plan, step, side):
         cols = columns(plan, step)
-        shares = FORWARD_ROWS[plan]
+        shares = FORWARD_ROWS[plan] if step < SHIFTED else (128, 128)
         rows = pl.ds(side * shares[0], shares[side])
         return remote(
             slabs.at[2 - side, rows, cols], slabs.at[3, rows, cols],
@@ -206,7 +207,7 @@
 
     def puts(unit):
         if unit == OWN:
-            for slot in range(7):
+            for slot in (0, 1, 2, 4, 5, 6):
                 move = (slot % 2, slot // 2 % 2)
                 band = [differ(bits[0], move[0]), differ(bits[1], move[1])]
                 yield move, differ(plane, slot // 4), band, plane, slot
@@ -244,6 +245,16 @@
                 yield remote(src, dst, put_send.at[unit, index], put_recv.at[unit], y_peers[move])
             elif with_local:
                 yield pltpu.make_async_copy(src, dst, put_recv.at[unit])
+
+    def chain_copy(side):
+        count = x_rows // 2
+        start = pl.multiple_of(core * core_rows + x * x_rows + side * count, count)
+        rows = pl.ds(start, count)
+        return remote(
+            weights.at[1 - side, rows, pl.ds((2 - side) * height, height)],
+            own_weights.at[rows, pl.ds(3 * height, height)],
+            chain_send.at[side], put_recv.at[OWN], y_peers[(side, 1 - side)],
+        )
 
     def x_copy(unit, side):
         region = x_region(unit, x, 0, x_rows)
@@ -309,6 +320,8 @@
     forward(2)
     for copy in put_copies(OWN, True):
         copy.start()
+    for side in range(2):
+        chain_copy(side).start()
     for unit in range(PLANS):
         x_end(unit)
     forward(3)
@@ -330,8 +343,7 @@
             result = term if result is None else result + term
         return result
 
-    @pl.loop(0, STEPS)
-    def _(step):
+    for step in range(STEPS):
         for plan in range(PLANS):
             cols = columns(plan, step)
             for side in range(2):
@@ -352,6 +364,8 @@
     for index in range(3):
         part_copy(index).wait_send()
     each(z_copies, "wait_send")
+    for side in range(2):
+        chain_copy(side).wait_send()
     each(zf_copies, "wait_send")
     for unit in range(PLANS + 1):
         for copy in put_copies(unit, False):
@@ -362,8 +376,7 @@
         for index in range(4):
             core_copy(unit, index).wait_send()
 
-    @pl.loop(0, STEPS)
-    def _(step):
+    for step in range(STEPS):
         for plan in range(PLANS):
             for side in range(2):
                 own_copy(plan, step, side).wait_send()
@@ -406,7 +419,7 @@
             dma((PLANS, STEPS, 2)), dma((PLANS, STEPS, 2)),
             dma((PLANS, STEPS, 2)), dma((PLANS, STEPS, 2)),
             dma((6,)), dma((2,)), dma((3,)), dma((3,)), dma((2, 2)), dma((2, 2)), dma((2, 2)), dma((2, 2)),
-            dma((PLANS + 1, 7)), dma((PLANS + 1,)),
+            dma((PLANS + 1, 7)), dma((PLANS + 1,)), dma((2,)),
             dma((PLANS + 1, 2)), dma((PLANS + 1, 2)),
             dma((PLANS + 1, 2)), dma((PLANS + 1, 2)),
             dma((PLANS + 1, 4)), dma((PLANS + 1, 4)),

time: 72.6 us -> 72.3 us (level)
  no operation moved by 1% of the time
where the time goes in v7:
time: 72.3 us; the launch traced here: 72.2 us
  Pallas kernels  70.5 us (98%)
  local copies, waits for them, and re-layouts  1.67 us (2%)
    pallas_call x1, Pallas kernels, shards(): pl.pallas_call(kernel, out_shape=pltpu.VMEM((block, width), BF16), in_spe...  70.5 us
    unnamed x1, local copies, waits for them, and re-layouts  1.67 us

profile of v7, /device:TPU:0, one launch (start us, length us, event | category | flops | bytes accessed | tf_op | source)
XLA Modules:
  0.0 72.2 jit_solution(3818459791162663501)
XLA Ops:
  0.0 70.5 %shard_map.73 = bf16[512,3072]{1,0:T(8,128)(2,1)S(1)} custom-call(s32[16]{0:T(128)} %assign_in.1, s32[16]{0:T(128)} %orders_in.1, s32[16]{0:T(128)} %offsets_in.1, f32[1,256]{1,0:T(1,128)} %bitcast.2, f32[1,256]{1,0:T(1,128)} %bitcast.3, bf16[256,256]{1,0:T(8,128)(2,1)} %right_in.1, bf16[256,3072]{1,0:T(8,128)(2,1)} %left.1), custom_call_target="tpu_custom_call" | custom-call | tf_op jit(solution)/shard_map/pallas_call | solution.py:402
  70.5 1.7 %copy.9 = bf16[512,3072]{1,0:T(8,128)(2,1)} copy(bf16[512,3072]{1,0:T(8,128)(2,1)S(1)} %shard_map.73) | data formatting | bytes 6291456

commit v8 on v7

--- a/solution.py
+++ b/solution.py
@@ -325,9 +325,9 @@
     for unit in range(PLANS):
         x_end(unit)
     forward(3)
+    x_begin(OWN)
     for unit in range(PLANS):
         core_end(unit)
-    x_begin(OWN)
     local.wait()
 
     def partner_product(plan, cols):
@@ -344,7 +344,7 @@
         return result
 
     for step in range(STEPS):
-        for plan in range(PLANS):
+        for plan in (2, 0, 1):
             cols = columns(plan, step)
             for side in range(2):
                 fwd_copy(plan, step, side).wait_recv()

time: 72.3 us -> 72.3 us (level)
  no operation moved by 1% of the time
where the time goes in v8:
time: 72.3 us; the launch traced here: 72.2 us
  Pallas kernels  70.5 us (98%)
  local copies, waits for them, and re-layouts  1.67 us (2%)
    pallas_call x1, Pallas kernels, shards(): pl.pallas_call(kernel, out_shape=pltpu.VMEM((block, width), BF16), in_spe...  70.5 us
    unnamed x1, local copies, waits for them, and re-layouts  1.67 us

profile of v8, /device:TPU:0, one launch (start us, length us, event | category | flops | bytes accessed | tf_op | source)
XLA Modules:
  0.0 72.2 jit_solution(8875671043004298286)
XLA Ops:
  0.0 70.5 %shard_map.73 = bf16[512,3072]{1,0:T(8,128)(2,1)S(1)} custom-call(s32[16]{0:T(128)} %assign_in.1, s32[16]{0:T(128)} %orders_in.1, s32[16]{0:T(128)} %offsets_in.1, f32[1,256]{1,0:T(1,128)} %bitcast.2, f32[1,256]{1,0:T(1,128)} %bitcast.3, bf16[256,256]{1,0:T(8,128)(2,1)} %right_in.1, bf16[256,3072]{1,0:T(8,128)(2,1)} %left.1), custom_call_target="tpu_custom_call" | custom-call | tf_op jit(solution)/shard_map/pallas_call | solution.py:402
  70.5 1.7 %copy.9 = bf16[512,3072]{1,0:T(8,128)(2,1)} copy(bf16[512,3072]{1,0:T(8,128)(2,1)S(1)} %shard_map.73) | data formatting | bytes 6291456
